TPU v7x, 256 devices: a whole 4x4x8 slice. The times are simulated.
256 devices in a mesh: seq: 16 (over x, y), head: 16 (over z, core).
Axes of the slice: x: 4, y: 4, z: 8, core: 2. Of those that a mesh axis runs over, the one named last changes fastest.
Arguments:
- layer_input: bfloat16 [8192, 4096], P('seq', 'head'), may hold values from -40 to 40
- qk_weight: bfloat16 [4096, 4096], P('seq', 'head'), may hold values from -0.09375 to 0.09375
- value_weight: bfloat16 [4096, 4096], P('seq', 'head'), may hold values from -0.09375 to 0.09375
- groups: int32 [2, 8192, 1], P(None, 'seq'), may hold values from 0 to 15; in each aligned block of 512 rows (0 to 511, 512 to 1023, ..., all dimensions but the last counted through in order) at most 48 rows name the same one
- buckets: int32 [2, 8192], P(None, 'seq'), may hold values from 0 to 7
- out_cotangent: bfloat16 [8192, 4096], P('seq', 'head'), may hold values from -6 to 6
Outputs:
- output: bfloat16 [8192, 4096], P('seq', 'head')
- input_grad: bfloat16 [8192, 4096], P('seq', 'head')
- qk_weight_grad: float32 [4096, 4096], P('seq', 'head')
- value_weight_grad: float32 [4096, 4096], P('seq', 'head')
Inputs may be any that keep to these rules, and one draw needn't show every extreme that they name: `groups`: among the 512 tokens of one device in one round no group is named more than 48 times, and in every draw some device's tokens name some group exactly 48 times.
All inputs are finite; a program needn't handle non-finite values.
Results may differ from a plain program's by a relative error of at most 0.018.
The roundings to bfloat16 on the way count: a program that leaves them out, or rounds other values in their place, can miss the bound.
Values may be sent and summed in bfloat16 or wider, within the bound.
A program may use at most 128 MiB of HBM per device.

v0:
```python
import math

import jax
import jax.numpy as jnp
from jax import lax
from jax.experimental import pallas as pl
from jax.experimental.pallas import tpu as pltpu
from jax.sharding import PartitionSpec as P

HEAD_DIM = 128
ROUNDS = 2
EPSILON = 1e-06
SELF_SCORE = -100000.0
MASKED_SCORE = -1000000000.0


MESH = pl.DeviceIdType.MESH
BF = jnp.bfloat16
F32 = jnp.float32


def rcopy(src, dst, ssem, rsem, dev):
    return pltpu.make_async_remote_copy(
        src_ref=src, dst_ref=dst, send_sem=ssem, recv_sem=rsem, device_id=dev, device_id_type=MESH
    )


class Sends:
    def __init__(self, sems):
        self.sems, self.used, self.open = sems, 0, []

    def start(self, src, dst, rsem, dev):
        copy = rcopy(src, dst, self.sems.at[self.used], rsem, dev)
        copy.start()
        self.used += 1
        self.open.append(copy)

    def finish(self):
        for copy in self.open:
            copy.wait_send()
        self.open = []


def arrived(ref, rsem, ssem, dev):
    rcopy(ref, ref, ssem, rsem, dev).wait_recv()


def place():
    s, h = lax.axis_index("seq"), lax.axis_index("head")
    return s, h, s // 4, s % 4, h // 2, h % 2


def enter(devices):
    barrier = pltpu.get_barrier_semaphore()
    for dev in devices:
        pl.semaphore_signal(barrier, inc=1, device_id=dev, device_id_type=MESH)
    pl.semaphore_wait(barrier, len(devices))


def ring_neighbours():
    s, h, x, y, z, c = place()
    east, west = (((x + 1) % 4) * 4 + y, h), (((x + 3) % 4) * 4 + y, h)
    north, south = (x * 4 + (y + 1) % 4, h), (x * 4 + (y + 3) % 4, h)
    up, down = (s, ((z + 1) % 8) * 2 + c), (s, ((z + 7) % 8) * 2 + c)
    twin = (s, 2 * z + 1 - c)
    return east, west, north, south, up, down, twin


def mm(a, b, ca, cb):
    return lax.dot_general(a, b, (((ca,), (cb,)), ((), ())), preferred_element_type=F32)


def iota(shape, axis):
    return lax.broadcasted_iota(jnp.int32, shape, axis).astype(F32)


def onehot(mask):
    return jnp.where(mask, 1.0, 0.0).astype(BF)


def split3(v):
    high = v.astype(BF).astype(F32)
    rest = v - high
    mid = rest.astype(BF).astype(F32)
    return high, mid, rest - mid


def pieces(v):
    return jnp.concatenate(split3(v), axis=0).astype(BF)


def fold3(v, n):
    return v[0:n] + v[n:2 * n] + v[2 * n:3 * n]


def key_factor(qf):
    mean = jnp.mean(qf * qf, axis=1, keepdims=True)
    return lax.rsqrt(mean + EPSILON) * (1.0 / math.sqrt(HEAD_DIM))


def whole_kernel(
    x_ref, wq_ref, wv_ref, dout, grow, brow,
    output, ig, gq, gv,
    xg, wg, dqv, dqvt,
    qv, pick, unpick, order, unorder, live, hot, rk,
    kbuf, kgot, sbuf, rbuf, dbuf, dgot, obuf, ogot, ggot, lbuf, lgot, mbuf, mgot,
    qs, ks, vs, ds_, probs, pairs, osum, vals, slots, dks, dvs, mixes,
    tme, ttwin, tgot, zgot, gsum, g1far, g1near, g2far, g2near,
    asend, arecv, ssem, zsem, tsem, w1sem, w2sem, rtsem, rzsem, s1sem, s2sem,
):
    s, h, x, y, z, c = place()
    east, west, north, south, up, down, twin = ring_neighbours()
    barrier = pltpu.get_barrier_semaphore()

    @pl.loop(1, 16)
    def _(k):
        pl.semaphore_signal(barrier, inc=1, device_id=((s + k) % 16, h), device_id_type=MESH)

    for dev in (up, down, twin):
        pl.semaphore_signal(barrier, inc=1, device_id=dev, device_id_type=MESH)
    pl.semaphore_wait(barrier, 18)
    out = Sends(ssem)

    def rows256(ref, k):
        return ref.at[pl.ds(256 * k, 256)]

    def post(n, src, dst):
        @pl.loop(1, 16)
        def _(k):
            d = (s + k) % 16
            rcopy(src.at[d], dst.at[s], asend.at[n], arecv.at[n], (d, h)).start()

        dst[s] = src[s]

    def collect(n, dst):
        part = dst.at[pl.ds(0, 15)]
        rcopy(part, part, asend.at[n], arecv.at[n], (s, h)).wait_recv()

    def sent(n, src):
        part = src.at[pl.ds(0, 15)]
        rcopy(part, part, asend.at[n], arecv.at[n], (s, h)).wait_send()

    first_axis = [(north, south), (east, west)]
    second_axis = [(east, west), (north, south)]
    prim, sec = [y, x], [x, y]
    own = [wq_ref, wv_ref]

    def wslot(j, p, r):
        return wg.at[r * 4 + p if j == 0 else p * 4 + r, j]

    def half(ref, k):
        return ref.at[pl.ds(128 * k, 128)]

    for j in (0, 1):
        plus, minus = first_axis[j]
        dst = wslot(j, prim[j], sec[j])
        out.start(own[j], dst, w1sem.at[j, 0], plus)
        out.start(own[j], dst, w1sem.at[j, 1], minus)
    for k in (0, 1):
        rows = pl.ds(256 * k, 256)
        out.start(x_ref.at[rows], xg.at[h, rows], zsem.at[0, 0, k], up)
        out.start(x_ref.at[rows], xg.at[h, rows], zsem.at[1, 0, k], down)

    def second_send(j, k, p, src):
        plus, minus = second_axis[j]
        dst = wslot(j, p, sec[j])
        out.start(src, dst, w2sem.at[j, k, 0], plus)
        out.start(src, dst, w2sem.at[j, k, 1], minus)

    for j in (0, 1):
        second_send(j, 0, prim[j], own[j])
    out.start(x_ref, xg.at[h], tsem.at[0, 0], twin)

    def first_arrivals(j):
        plus, minus = first_axis[j]
        for k, (step, onward) in enumerate(((3, plus), (1, minus))):
            p = (prim[j] + step) % 4
            ref = wslot(j, p, sec[j])
            arrived(ref, w1sem.at[j, k], ssem.at[0], plus)
            out.start(half(ref, k), half(ref, k), w1sem.at[j, 2 + k], onward)
            second_send(j, 1 + k, p, ref)

    def first_far(j):
        p = (prim[j] + 2) % 4
        ref = wslot(j, p, sec[j])
        for k in (0, 1):
            arrived(half(ref, k), w1sem.at[j, 2 + k], ssem.at[0], first_axis[j][0])
        second_send(j, 3, p, ref)

    offsets = (0, 3, 1, 2)

    def second_arrivals(j, k):
        p = (prim[j] + offsets[k]) % 4
        plus, minus = second_axis[j]
        for side, (step, onward) in enumerate(((3, plus), (1, minus))):
            ref = wslot(j, p, (sec[j] + step) % 4)
            arrived(ref, w2sem.at[j, k, side], ssem.at[0], plus)
            out.start(half(ref, side), half(ref, side), w2sem.at[j, k, 2 + side], onward)

    def second_far(j, k):
        p = (prim[j] + offsets[k]) % 4
        ref = wslot(j, p, (sec[j] + 2) % 4)
        for side in (0, 1):
            arrived(half(ref, side), w2sem.at[j, k, 2 + side], ssem.at[0], second_axis[j][0])

    def z_arrival(dist):
        for k in (0, 1):
            for side, (step, onward) in enumerate(((8 - dist, up), (dist, down))):
                ref = rows256(xg.at[((z + step) % 8) * 2 + c], k)
                arrived(ref, zsem.at[side, dist - 1, k], ssem.at[0], up)
                if dist < 3 or k == side:
                    out.start(ref, ref, zsem.at[side, dist, k], onward)
        for side, step in enumerate((8 - dist, dist)):
            ref = xg.at[((z + step) % 8) * 2 + c]
            out.start(ref, ref, tsem.at[side, dist], twin)

    def z_far():
        ref = xg.at[((z + 4) % 8) * 2 + c]
        for side in (0, 1):
            arrived(rows256(ref, side), zsem.at[side, 3, side], ssem.at[0], up)
            out.start(rows256(ref, side), rows256(ref, side), tsem.at[side, 4], twin)

    def twin_arrivals():
        arrived(xg.at[2 * z + 1 - c], tsem.at[0, 0], ssem.at[0], twin)
        for dist in (1, 2, 3):
            for side, step in enumerate((8 - dist, dist)):
                arrived(xg.at[((z + step) % 8) * 2 + 1 - c], tsem.at[side, dist], ssem.at[0], twin)
        for side in (0, 1):
            ref = xg.at[((z + 4) % 8) * 2 + 1 - c]
            arrived(rows256(ref, side), tsem.at[side, 4], ssem.at[0], twin)

    xg[h] = x_ref[...]
    wg[s, 0] = wq_ref[...]
    wg[s, 1] = wv_ref[...]

    kbuf[...] = jnp.zeros_like(kbuf)
    lbuf[...] = jnp.zeros_like(lbuf)
    vals[...] = jnp.zeros_like(vals)
    slots[...] = jnp.zeros_like(slots)
    upper = onehot(iota((512, 512), 0) <= iota((512, 512), 1))
    eye = iota((512, 512), 0) == iota((512, 512), 1)
    slot_rows, slot_cols = [], []
    for t in (0, 1):
        g = grow[t].astype(F32)
        member = jnp.where(iota((16, 512), 0) == g, 1.0, 0.0)
        count = mm(member.astype(BF), upper, 1, 0)
        rank = jnp.sum(member * count, axis=0, keepdims=True) - 1.0
        slot = g * 48.0 + rank
        slot_col = jnp.sum(jnp.where(eye, slot, 0.0), axis=1, keepdims=True)
        hot[t] = member
        rk[t] = onehot(iota((128, 512), 0) == rank)
        slot_rows.append(slot)
        slot_cols.append(slot_col)
        named = member * (brow[t:t + 1, :].astype(F32) + 1.0)
        sent_keys = mm(named.astype(BF), rk[t], 1, 1)
        for d in range(16):
            kbuf[d, t:t + 1, :] = sent_keys[d:d + 1, :]
    post(0, kbuf, kgot)

    def slot_order(t):
        tag = jnp.concatenate([kgot[d, t:t + 1, :] for d in range(16)], axis=0)
        usable = iota((16, 128), 1) < 48.0
        kinds = [jnp.where(tag == float(k), 1.0, 0.0) for k in range(1, 9)]
        kinds.append(jnp.where(usable, jnp.where(tag == 0.0, 1.0, 0.0), 0.0))
        stack = jnp.concatenate(kinds, axis=0)
        within = mm(stack.astype(BF), onehot(iota((128, 128), 0) <= iota((128, 128), 1)), 1, 0)
        totals = jnp.broadcast_to(within[:, 127:128], (144, 128)).astype(BF)
        before = mm(onehot(iota((144, 144), 0) > iota((144, 144), 1)), totals, 1, 0)
        place_all = stack * (within + before - 1.0)
        rank = place_all[0:16]
        for k in range(1, 9):
            rank = rank + place_all[16 * k:16 * (k + 1)]
        live[t] = before[128:136, :]
        small_eye = iota((48, 128), 0) == iota((48, 128), 1)
        columns = jnp.concatenate(
            [
                jnp.sum(jnp.where(small_eye, rank[d:d + 1, :], 0.0), axis=1, keepdims=True)
                for d in range(16)
            ],
            axis=0,
        )
        unorder[t] = onehot(iota((768, 768), 1) == columns)
        row = jnp.sum(
            jnp.where(iota((768, 768), 0) == iota((768, 768), 1), columns, 0.0),
            axis=0, keepdims=True,
        )
        order[t] = onehot(iota((768, 768), 0) == row)

    for j in (0, 1):
        first_arrivals(j)
    for j in (0, 1):
        second_arrivals(j, 0)
    z_arrival(1)
    pick[0] = onehot(iota((768, 512), 0) == slot_rows[0])
    for j in (0, 1):
        first_far(j)
    for j in (0, 1):
        second_arrivals(j, 1)
    z_arrival(2)
    pick[1] = onehot(iota((768, 512), 0) == slot_rows[1])
    for t in (0, 1):
        dbuf[:, t] = mm(pick[t], dout[...], 1, 0).astype(BF).reshape(16, 48, 256)
    post(5, dbuf, dgot)

    for t in (0, 1):
        unpick[:, 768 * t:768 * (t + 1)] = onehot(iota((512, 768), 1) == slot_cols[t])
    for j in (0, 1):
        second_arrivals(j, 2)
    z_arrival(3)
    collect(0, kgot)
    slot_order(0)
    for j in (0, 1):
        second_arrivals(j, 3)
    z_far()
    slot_order(1)
    for k in range(4):
        second_far(0, k)
        second_far(1, k)
    twin_arrivals()

    for j in (0, 1):
        probs[j, 0:4] = jnp.zeros((4, 128, 256), F32)

    @pl.loop(0, 4)
    def _(i):
        for j in (0, 1):
            total = probs[j, 0:4].reshape(512, 256)
            for k in range(4):
                b = 4 * i + k
                total += mm(xg[b], wg[b, j], 1, 0)
            probs[j, 0:4] = total.reshape(4, 128, 256)

    for j in (0, 1):
        for n in (0, 1):
            part = probs[j, 0:4, :, 128 * n:128 * (n + 1)].reshape(512, 128)
            qv[n, :, 128 * j:128 * (j + 1)] = part.astype(BF)

    for n in (0, 1):
        for t in (0, 1):
            sbuf[n, t] = mm(pick[t], qv[n], 1, 0).astype(BF).reshape(16, 48, 256)
            post(1 + 2 * n + t, sbuf.at[n, t], rbuf.at[n, t])
    def both(ref, lead, b):
        prev = (b + 5) % 6
        return jnp.concatenate(
            [ref[lead, 128 * b:128 * (b + 1)], ref[lead, 128 * prev:128 * (prev + 1)]], axis=0
        )

    self_pair = iota((128, 256), 0) == iota((128, 256), 1)

    collect(5, dgot)

    @pl.loop(0, 2)
    def _(t):
        rows = mm(order[t], dgot[:, t].reshape(768, 256), 1, 0).astype(BF)
        ds_[t] = rows[:, 0:128]
        ds_[2 + t] = rows[:, 128:256]

    choose = onehot(iota((8, 128), 0) == iota((8, 128), 1))

    for n in (0, 1):

        @pl.loop(0, 2)
        def _(t):
            u = 2 * n + t
            collect(1 + u, rbuf.at[n, t])
            rows = mm(order[t], rbuf[n, t].reshape(768, 256), 1, 0)
            qf = rows[:, 0:128]
            fac = key_factor(qf)
            qs[u] = qf.astype(BF)
            ks[u] = (qf * fac).astype(BF)
            vs[u] = rows[:, 128:256].astype(BF)
            for b in range(6):
                prev = (b + 5) % 6
                at = iota((1, 256), 1)
                at = jnp.where(at < 128.0, at + 128.0 * b, at - 128.0 + 128.0 * prev)
                used = jnp.concatenate([live[t, 0:1, :]] * 2, axis=1)
                scores = mm(qs[u, 128 * b:128 * (b + 1)], both(ks, u, b), 1, 1)
                scores = jnp.where(self_pair, SELF_SCORE, scores)
                scores = jnp.where(at < used, scores, MASKED_SCORE)
                top = jnp.max(scores, axis=1, keepdims=True)
                e = jnp.exp(scores - top)
                total = jnp.sum(e, axis=1, keepdims=True)
                weights = e * (1.0 / total)
                probs[u, b] = weights
                mixed = mm(weights.astype(BF), both(vs, u, b), 1, 0)
                osum[u, 128 * b:128 * (b + 1)] = mixed
                grad = ds_[u, 128 * b:128 * (b + 1)]
                pairs[u, b] = mm(grad, both(vs, u, b), 1, 1)
                vals[t, 128 * b:128 * (b + 1), 2 + n:3 + n] = jnp.sum(
                    grad.astype(F32) * mixed, axis=1, keepdims=True
                )
                vals[t, 128 * b:128 * (b + 1), n:n + 1] = top + jnp.log(total)
            if n == 1:
                high, mid, low = split3(vals[t])
                lines = pieces(
                    mm(choose, high.astype(BF), 1, 1)
                    + mm(choose, mid.astype(BF), 1, 1)
                    + mm(choose, low.astype(BF), 1, 1)
                )
                for d in range(16):
                    lbuf[d, pl.ds(pl.multiple_of(8 * t, 8), 8), 0:48] = fold3(
                        mm(lines, unorder[t, 48 * d:48 * (d + 1)], 1, 1), 8
                    )

    post(6, lbuf, lgot)
    for t in (0, 1):
        wide = jnp.concatenate([osum[t], osum[2 + t]], axis=1).astype(BF)
        obuf[:, t] = mm(unorder[t], wide, 1, 0).astype(BF).reshape(16, 48, 256)
    post(7, obuf, ogot)

    collect(6, lgot)
    here = []
    for t in (0, 1):
        high, mid, low = split3(lgot[:, 8 * t:8 * (t + 1), :].reshape(128, 128))
        found = (
            mm(high.astype(BF), rk[t], 1, 0)
            + mm(mid.astype(BF), rk[t], 1, 0)
            + mm(low.astype(BF), rk[t], 1, 0)
        )
        line = found[0:8] * hot[t, 0:1, :]
        for g in range(1, 16):
            line = line + found[8 * g:8 * (g + 1)] * hot[t, g:g + 1, :]
        here.append(line)
    top = jnp.maximum(here[0], here[1])
    log_all = top + jnp.log(jnp.exp(here[0] - top) + jnp.exp(here[1] - top))
    mix = [jnp.exp(line - log_all) for line in here]
    inner = mix[0][0:2] * here[0][2:4] + mix[1][0:2] * here[1][2:4]
    mix_lines = []
    for t in (0, 1):
        lines = jnp.concatenate([mix[t][0:2], inner, jnp.zeros((4, 512), F32)], axis=0)
        split = jnp.concatenate(split3(lines), axis=0)
        stack = jnp.concatenate([split * hot[t, g:g + 1, :] for g in range(16)], axis=0)
        back = mm(stack.astype(BF), rk[t], 1, 1)
        for g in range(16):
            mbuf[g, 8 * t:8 * (t + 1), :] = fold3(back[24 * g:24 * (g + 1)], 8)
        mix_lines.append(split)
    post(8, mbuf, mgot)
    for t in (0, 1):
        mixes[t] = mm(onehot(eye), mix_lines[t].astype(BF), 1, 1)

    collect(8, mgot)
    lane_eye = onehot(iota((48, 128), 0) == iota((48, 128), 1))
    for t in (0, 1):
        for d in range(16):
            slots[t, 48 * d:48 * (d + 1), 0:24] = mm(
                lane_eye, pieces(mgot[d, 8 * t:8 * (t + 1), :]), 1, 1
            ).astype(BF)
        vals[t] = mm(order[t], slots[t], 1, 0)

    def column(ref, t, j):
        return ref[t, :, j:j + 1] + ref[t, :, 8 + j:9 + j] + ref[t, :, 16 + j:17 + j]

    for n in (0, 1):

        @pl.loop(0, 2)
        def _(t):
            u = 2 * n + t
            sent(1 + u, sbuf.at[n, t])
            mix_col = column(vals, t, n)
            inner_col = column(vals, t, 2 + n)
            dks[...] = jnp.zeros_like(dks)
            dvs[...] = jnp.zeros_like(dvs)
            dq = []
            for b in range(6):
                prev = (b + 5) % 6
                rows = slice(128 * b, 128 * (b + 1))
                prows = slice(128 * prev, 128 * (prev + 1))
                weighted = probs[u, b] * mix_col[rows]
                grads = jnp.where(self_pair, 0.0, weighted * (pairs[u, b] - inner_col[rows]))
                grads = grads.astype(BF)
                dq.append(mm(grads, both(ks, u, b), 1, 0))
                dk = mm(grads, qs[u, rows], 0, 0)
                dv = mm(weighted.astype(BF), ds_[u, rows], 0, 0)
                dks[rows] += dk[0:128]
                dks[prows] += dk[128:256]
                dvs[rows] += dv[0:128]
                dvs[prows] += dv[128:256]
            qf = qs[u].astype(F32)
            fac = key_factor(qf)
            dk = dks[...]
            inside = jnp.sum(dk * qf, axis=1, keepdims=True)
            result = jnp.concatenate(dq, axis=0) + fac * dk - fac * fac * fac * inside * qf
            wide = jnp.concatenate([result.astype(BF), dvs[...].astype(BF)], axis=1)
            sbuf[n, t] = mm(unorder[t], wide, 1, 0).astype(BF).reshape(16, 48, 256)
            post(9 + u, sbuf.at[n, t], ggot.at[n, t])

    collect(7, ogot)
    parts = [mm(unpick[:, 768 * t:768 * (t + 1)], ogot[:, t].reshape(768, 256), 1, 0) for t in (0, 1)]
    for n in (0, 1):
        lanes = slice(128 * n, 128 * (n + 1))
        output[:, lanes] = (
            column(mixes, 0, n) * parts[0][:, lanes] + column(mixes, 1, n) * parts[1][:, lanes]
        ).astype(BF)

    for n in (0, 1):
        collect(9 + 2 * n, ggot.at[n, 0])
        rows = mm(unpick[:, 0:768], ggot[n, 0].reshape(768, 256), 1, 0)
        collect(10 + 2 * n, ggot.at[n, 1])
        rows = rows + mm(unpick[:, 768:1536], ggot[n, 1].reshape(768, 256), 1, 0)
        rows = rows.astype(BF)
        dqv[:, 128 * n:128 * (n + 1)] = rows[:, 0:128]
        dqv[:, 256 + 128 * n:256 + 128 * (n + 1)] = rows[:, 128:256]
        dqvt[128 * n:128 * (n + 1), :] = jnp.transpose(rows[:, 0:128])
        dqvt[256 + 128 * n:256 + 128 * (n + 1), :] = jnp.transpose(rows[:, 128:256])

    def term(b):
        return mm(dqv[:, 0:256], wg[b, 0], 1, 1) + mm(dqv[:, 256:512], wg[b, 1], 1, 1)

    def twin_term(k, zd):
        ttwin[zd] = term(2 * zd + 1 - c).astype(BF)
        out.start(ttwin.at[zd], tgot.at[zd], rtsem.at[k], twin)

    def my_term(zd):
        tme[zd] = term(2 * zd + c).astype(BF)

    def pair(k, zd):
        arrived(tgot.at[zd], rtsem.at[k], ssem.at[0], twin)
        tme[zd] = (tme[zd].astype(F32) + tgot[zd].astype(F32)).astype(BF)

    prim, sec = [x, y], [y, x]
    first_axis = [(east, west), (north, south)]
    second_axis = [(north, south), (east, west)]

    def grads(j, r):
        @pl.loop(0, 4)
        def _(p):
            b = r * 4 + p if j == 0 else p * 4 + r
            gsum[j, r, p] = mm(dqvt[256 * j:256 * (j + 1), :], xg[b], 1, 0).astype(BF)

    order = (2, 1, 3, 0)

    def first_far_send(j):
        r = (prim[j] + 2) % 4
        for k, off in enumerate(order):
            p = (sec[j] + off) % 4
            for side in (0, 1):
                out.start(
                    half(gsum.at[j, r, p], side), g1far.at[j, side, p], s1sem.at[j, k, side],
                    first_axis[j][side],
                )

    def first_near_send(j):
        for k, off in enumerate(order):
            p = (sec[j] + off) % 4
            for side, step in enumerate((1, 3)):
                r = (prim[j] + step) % 4
                arrived(g1far.at[j, side, p], s1sem.at[j, k, side], ssem.at[0], first_axis[j][0])
                rows = pl.ds(128 * side, 128)
                gsum[j, r, p, rows] = (
                    gsum[j, r, p, rows].astype(F32) + g1far[j, side, p].astype(F32)
                ).astype(BF)
                out.start(
                    gsum.at[j, r, p], g1near.at[j, side, p], s1sem.at[j, k, 2 + side],
                    first_axis[j][side],
                )

    def first_final(j, k):
        p = (sec[j] + order[k]) % 4
        for side in (0, 1):
            arrived(g1near.at[j, side, p], s1sem.at[j, k, 2 + side], ssem.at[0], first_axis[j][0])
        r = prim[j]
        gsum[j, r, p] = (
            gsum[j, r, p].astype(F32) + g1near[j, 0, p].astype(F32) + g1near[j, 1, p].astype(F32)
        ).astype(BF)

    def second_far_send(j):
        p = (sec[j] + 2) % 4
        for side in (0, 1):
            out.start(
                half(gsum.at[j, prim[j], p], side), g2far.at[j, side], s2sem.at[j, side],
                second_axis[j][side],
            )

    def second_near_send(j):
        for side, step in enumerate((1, 3)):
            p = (sec[j] + step) % 4
            arrived(g2far.at[j, side], s2sem.at[j, side], ssem.at[0], second_axis[j][0])
            rows = pl.ds(128 * side, 128)
            gsum[j, prim[j], p, rows] = (
                gsum[j, prim[j], p, rows].astype(F32) + g2far[j, side].astype(F32)
            ).astype(BF)
            out.start(
                gsum.at[j, prim[j], p], g2near.at[j, side], s2sem.at[j, 2 + side],
                second_axis[j][side],
            )

    def second_final(j, result):
        for side in (0, 1):
            arrived(g2near.at[j, side], s2sem.at[j, 2 + side], ssem.at[0], second_axis[j][0])
        result[...] = jnp.transpose(
            gsum[j, prim[j], sec[j]].astype(F32)
            + g2near[j, 0].astype(F32)
            + g2near[j, 1].astype(F32)
        )

    def z_send(step):
        if step == 0:
            zd = (z + 4) % 8
            for side, onward in enumerate((up, down)):
                out.start(
                    rows256(tme.at[zd], side), rows256(zgot.at[side, 0], side), rzsem.at[side, 0],
                    onward,
                )
            return
        for side, (zd, onward) in enumerate((((z + 4 - step) % 8, up), ((z + 4 + step) % 8, down))):
            if step == 1:
                rows = pl.ds(256 * side, 256)
                arrived(zgot.at[side, 0, rows], rzsem.at[side, 0], ssem.at[0], up)
                tme[zd, rows] = (
                    tme[zd, rows].astype(F32) + zgot[side, 0, rows].astype(F32)
                ).astype(BF)
            else:
                arrived(zgot.at[side, step - 1], rzsem.at[side, step - 1], ssem.at[0], up)
                tme[zd] = (tme[zd].astype(F32) + zgot[side, step - 1].astype(F32)).astype(BF)
            out.start(tme.at[zd], zgot.at[side, step], rzsem.at[side, step], onward)

    zorder = [(z + off) % 8 for off in (4, 3, 5, 2, 6, 1, 7, 0)]

    twin_term(0, zorder[0])
    for j in (0, 1):
        grads(j, (prim[j] + 2) % 4)
        first_far_send(j)
    my_term(zorder[0])
    pair(0, zorder[0])
    z_send(0)
    for k in (1, 2):
        twin_term(k, zorder[k])
        my_term(zorder[k])
    for j in (0, 1):
        grads(j, (prim[j] + 1) % 4)
        grads(j, (prim[j] + 3) % 4)
        first_near_send(j)
    pair(1, zorder[1])
    pair(2, zorder[2])
    z_send(1)
    for k in (3, 4, 5, 6, 7):
        twin_term(k, zorder[k])
        my_term(zorder[k])
    for j in (0, 1):
        grads(j, prim[j])
    pair(3, zorder[3])
    pair(4, zorder[4])
    z_send(2)
    for j in (0, 1):
        first_final(j, 0)
        second_far_send(j)
    pair(5, zorder[5])
    pair(6, zorder[6])
    z_send(3)
    for j in (0, 1):
        first_final(j, 1)
        first_final(j, 2)
        second_near_send(j)
        first_final(j, 3)
    pair(7, zorder[7])
    for side in (0, 1):
        arrived(zgot.at[side, 3], rzsem.at[side, 3], ssem.at[0], up)
    ig[...] = (
        tme[z].astype(F32) + zgot[0, 3].astype(F32) + zgot[1, 3].astype(F32)
    ).astype(BF)
    second_final(0, gq)
    second_final(1, gv)
    out.finish()
    sent(0, kbuf)
    for u in range(4):
        sent(9 + u, sbuf.at[u // 2, u % 2])
    sent(5, dbuf)
    sent(6, lbuf)
    sent(7, obuf)
    sent(8, mbuf)


def copy_kernel(*refs):
    for source, target in zip(refs[0:4], refs[4:8]):
        target[...] = source[...]


def per_device(layer_input, qk_weight, value_weight, groups, buckets, out_cotangent):
    vm = pl.BlockSpec(memory_space=pltpu.VMEM)
    V = pltpu.VMEM
    shapes = (
        jax.ShapeDtypeStruct((512, 256), BF),
        jax.ShapeDtypeStruct((512, 256), BF),
        jax.ShapeDtypeStruct((256, 256), F32),
        jax.ShapeDtypeStruct((256, 256), F32),
    )
    results = pl.pallas_call(
        whole_kernel,
        out_shape=shapes,
        in_specs=[vm] * 6,
        out_specs=(vm,) * 4,
        scratch_shapes=[
            V((16, 512, 256), BF),
            V((16, 2, 256, 256), BF),
            V((512, 512), BF),
            V((512, 512), BF),
            V((2, 512, 256), BF),
            V((2, 768, 512), BF),
            V((512, 1536), BF),
            V((2, 768, 768), BF),
            V((2, 768, 768), BF),
            V((2, 8, 128), F32),
            V((2, 16, 512), F32),
            V((2, 128, 512), BF),
            V((16, 8, 128), F32),
            V((16, 8, 128), F32),
            V((2, 2, 16, 48, 256), BF),
            V((2, 2, 16, 48, 256), BF),
            V((16, 2, 48, 256), BF),
            V((16, 2, 48, 256), BF),
            V((16, 2, 48, 256), BF),
            V((16, 2, 48, 256), BF),
            V((2, 2, 16, 48, 256), BF),
            V((16, 16, 128), F32),
            V((16, 16, 128), F32),
            V((16, 16, 128), F32),
            V((16, 16, 128), F32),
            V((4, 768, 128), BF),
            V((4, 768, 128), BF),
            V((4, 768, 128), BF),
            V((4, 768, 128), BF),
            V((4, 6, 128, 256), F32),
            V((4, 6, 128, 256), F32),
            V((4, 768, 128), F32),
            V((2, 768, 128), F32),
            V((2, 768, 128), BF),
            V((768, 128), F32),
            V((768, 128), F32),
            V((2, 512, 24), F32),
            V((8, 512, 256), BF),
            V((8, 512, 256), BF),
            V((8, 512, 256), BF),
            V((2, 4, 512, 256), BF),
            V((2, 4, 4, 256, 256), BF),
            V((2, 2, 4, 128, 256), BF),
            V((2, 2, 4, 256, 256), BF),
            V((2, 2, 128, 256), BF),
            V((2, 2, 256, 256), BF),
            pltpu.SemaphoreType.DMA((13,)),
            pltpu.SemaphoreType.DMA((13,)),
            pltpu.SemaphoreType.DMA((160,)),
            pltpu.SemaphoreType.DMA((2, 4, 2)),
            pltpu.SemaphoreType.DMA((2, 5)),
            pltpu.SemaphoreType.DMA((2, 4)),
            pltpu.SemaphoreType.DMA((2, 4, 4)),
            pltpu.SemaphoreType.DMA((8,)),
            pltpu.SemaphoreType.DMA((2, 4)),
            pltpu.SemaphoreType.DMA((2, 4, 4)),
            pltpu.SemaphoreType.DMA((2, 4)),
        ],
        compiler_params=pltpu.CompilerParams(
            collective_id=0, has_side_effects=True, vmem_limit_bytes=63 * 1024 * 1024
        ),
        name="hashed_attention_step",
    )(layer_input, qk_weight, value_weight, out_cotangent, jnp.transpose(groups, (0, 2, 1)), buckets)
    return pl.pallas_call(
        copy_kernel,
        out_shape=shapes,
        in_specs=[vm] * 4,
        out_specs=(vm,) * 4,
        name="write_results",
    )(*results)


def solution(mesh):
    return jax.shard_map(
        per_device,
        mesh=mesh,
        in_specs=(
            P("seq", "head"),
            P("seq", "head"),
            P("seq", "head"),
            P(None, "seq", None),
            P(None, "seq"),
            P("seq", "head"),
        ),
        out_specs=(P("seq", "head"), P("seq", "head"), P("seq", "head"), P("seq", "head")),
        check_vma=False,
    )
```

profile of v0, /device:TPU:8, one launch (start us, length us, event | category | flops | bytes accessed | tf_op | source)
XLA Modules:
  0.0 142.7 jit_solution(5842838237843670325)
XLA Ops:
  0.6 139.9 %hashed_attention_step.1 = (bf16[512,256]{1,0:T(8,128)(2,1)}, bf16[512,256]{1,0:T(8,128)(2,1)}, f32[256,256]{1,0:T(8,128)}, f32[256,256]{1,0:T(8,128)}) custom-call(bf16[512,256]{1,0:T(8,128)(2,1)} %x_ref.1, bf16[256,256]{1,0:T(8,128)(2,1)} %wq_ref.1, bf16[256,256]{1,0:T(8,128)(2,1)} %wv_ref.1, bf16[512,256]{1,0:T(8,128)(2,1)} %dout.1, ...), custom_call_target="tpu_custom_call" | custom-call | tf_op jit(solution)/shard_map/hashed_attention_step/pallas_call | solution.py:687
  140.6 2.2 %write_results.1 = (bf16[512,256]{1,0:T(8,128)(2,1)}, bf16[512,256]{1,0:T(8,128)(2,1)}, f32[256,256]{1,0:T(8,128)}, f32[256,256]{1,0:T(8,128)}) custom-call(bf16[512,256]{1,0:T(8,128)(2,1)} %get-tuple-element.8.refs_0_, bf16[512,256]{1,0:T(8,128)(2,1)} %get-tuple-element.9.refs_1_, f32[256,256]{1,0:T(8,128)} %get-tuple-element.10.refs_2_, ...), custom_call_target="tpu_custom_call" | custom-call | tf_op jit(solution)/shard_map/write_results/pallas_call | solution.py:756
where the time goes:
time: 143 us
  Pallas kernels  142 us (99%)
    pallas_call x1, Pallas kernels, per_device(): pl.pallas_call(whole_kernel, out_shape=shapes, in_specs=[vm] * 6, out_spe...  140 us

commit v1 on v0

--- a/solution.py
+++ b/solution.py
@@ -225,6 +225,8 @@
         for dist in (1, 2, 3):
             for side, step in enumerate((8 - dist, dist)):
                 arrived(xg.at[((z + step) % 8) * 2 + 1 - c], tsem.at[side, dist], ssem.at[0], twin)
+
+    def twin_far():
         for side in (0, 1):
             ref = xg.at[((z + 4) % 8) * 2 + 1 - c]
             arrived(rows256(ref, side), tsem.at[side, 4], ssem.at[0], twin)
@@ -239,8 +241,11 @@
     slots[...] = jnp.zeros_like(slots)
     upper = onehot(iota((512, 512), 0) <= iota((512, 512), 1))
     eye = iota((512, 512), 0) == iota((512, 512), 1)
+    for j in (0, 1):
+        probs[j, 0:4] = jnp.zeros((4, 128, 256), F32)
     slot_rows, slot_cols = [], []
-    for t in (0, 1):
+
+    def token_layout(t):
         g = grow[t].astype(F32)
         member = jnp.where(iota((16, 512), 0) == g, 1.0, 0.0)
         count = mm(member.astype(BF), upper, 1, 0)
@@ -255,7 +260,7 @@
         sent_keys = mm(named.astype(BF), rk[t], 1, 1)
         for d in range(16):
             kbuf[d, t:t + 1, :] = sent_keys[d:d + 1, :]
-    post(0, kbuf, kgot)
+    token_layout(0)
 
     def slot_order(t):
         tag = jnp.concatenate([kgot[d, t:t + 1, :] for d in range(16)], axis=0)
@@ -288,6 +293,8 @@
 
     for j in (0, 1):
         first_arrivals(j)
+    token_layout(1)
+    post(0, kbuf, kgot)
     for j in (0, 1):
         second_arrivals(j, 0)
     z_arrival(1)
@@ -300,7 +307,6 @@
     pick[1] = onehot(iota((768, 512), 0) == slot_rows[1])
     for t in (0, 1):
         dbuf[:, t] = mm(pick[t], dout[...], 1, 0).astype(BF).reshape(16, 48, 256)
-    post(5, dbuf, dgot)
 
     for t in (0, 1):
         unpick[:, 768 * t:768 * (t + 1)] = onehot(iota((512, 768), 1) == slot_cols[t])
@@ -311,6 +317,7 @@
     slot_order(0)
     for j in (0, 1):
         second_arrivals(j, 3)
+    post(5, dbuf, dgot)
     z_far()
     slot_order(1)
     for k in range(4):
@@ -318,18 +325,19 @@
         second_far(1, k)
     twin_arrivals()
 
-    for j in (0, 1):
-        probs[j, 0:4] = jnp.zeros((4, 128, 256), F32)
-
-    @pl.loop(0, 4)
-    def _(i):
+    def project(q):
+        chip = (z + 5 + q) % 8
         for j in (0, 1):
-            total = probs[j, 0:4].reshape(512, 256)
-            for k in range(4):
-                b = 4 * i + k
-                total += mm(xg[b], wg[b, j], 1, 0)
-            probs[j, 0:4] = total.reshape(4, 128, 256)
-
+            total = mm(xg[2 * chip], wg[2 * chip, j], 1, 0)
+            total += mm(xg[2 * chip + 1], wg[2 * chip + 1, j], 1, 0)
+            probs[j, 0:4] += total.reshape(4, 128, 256)
+
+    @pl.loop(0, 7)
+    def _(q):
+        project(q)
+
+    twin_far()
+    project(7)
     for j in (0, 1):
         for n in (0, 1):
             part = probs[j, 0:4, :, 128 * n:128 * (n + 1)].reshape(512, 128)
@@ -521,43 +529,59 @@
     first_axis = [(east, west), (north, south)]
     second_axis = [(north, south), (east, west)]
 
-    def grads(j, r):
+    def grads(j, off):
+        p = (sec[j] + off) % 4
+
+        @pl.loop(1, 4)
+        def _(i):
+            r = (prim[j] + i) % 4
+            b = r * 4 + p if j == 0 else p * 4 + r
+            gsum[j, r, p] = mm(dqvt[256 * j:256 * (j + 1), :], xg[b], 1, 0).astype(BF)
+
+    def own_grads(j):
         @pl.loop(0, 4)
         def _(p):
+            r = prim[j]
             b = r * 4 + p if j == 0 else p * 4 + r
             gsum[j, r, p] = mm(dqvt[256 * j:256 * (j + 1), :], xg[b], 1, 0).astype(BF)
 
-    order = (2, 1, 3, 0)
-
-    def first_far_send(j):
+    offs = (2, 1, 3, 0)
+
+    def add(ref, index, other):
+        ref[index] = (ref[index].astype(F32) + other.astype(F32)).astype(BF)
+
+    def first_sends(j, k):
+        p = (sec[j] + offs[k]) % 4
         r = (prim[j] + 2) % 4
-        for k, off in enumerate(order):
-            p = (sec[j] + off) % 4
-            for side in (0, 1):
-                out.start(
-                    half(gsum.at[j, r, p], side), g1far.at[j, side, p], s1sem.at[j, k, side],
-                    first_axis[j][side],
-                )
-
-    def first_near_send(j):
-        for k, off in enumerate(order):
-            p = (sec[j] + off) % 4
-            for side, step in enumerate((1, 3)):
-                r = (prim[j] + step) % 4
-                arrived(g1far.at[j, side, p], s1sem.at[j, k, side], ssem.at[0], first_axis[j][0])
-                rows = pl.ds(128 * side, 128)
-                gsum[j, r, p, rows] = (
-                    gsum[j, r, p, rows].astype(F32) + g1far[j, side, p].astype(F32)
-                ).astype(BF)
-                out.start(
-                    gsum.at[j, r, p], g1near.at[j, side, p], s1sem.at[j, k, 2 + side],
-                    first_axis[j][side],
-                )
+        for side in (0, 1):
+            out.start(
+                half(gsum.at[j, r, p], side), g1far.at[j, side, p], s1sem.at[j, k, side],
+                first_axis[j][side],
+            )
+        for side, step in enumerate((1, 3)):
+            r = (prim[j] + step) % 4
+            out.start(
+                half(gsum.at[j, r, p], 1 - side), half(g1near.at[j, side, p], 1 - side),
+                s1sem.at[j, k, 2 + side], first_axis[j][side],
+            )
+
+    def first_relay(j, k):
+        p = (sec[j] + offs[k]) % 4
+        for side, step in enumerate((1, 3)):
+            r = (prim[j] + step) % 4
+            arrived(g1far.at[j, side, p], s1sem.at[j, k, side], ssem.at[0], first_axis[j][0])
+            add(gsum, (j, r, p, pl.ds(128 * side, 128)), g1far[j, side, p])
+            out.start(
+                half(gsum.at[j, r, p], side), half(g1near.at[j, side, p], side),
+                s1sem.at[j, k, 4 + side], first_axis[j][side],
+            )
 
     def first_final(j, k):
-        p = (sec[j] + order[k]) % 4
+        p = (sec[j] + offs[k]) % 4
         for side in (0, 1):
-            arrived(g1near.at[j, side, p], s1sem.at[j, k, 2 + side], ssem.at[0], first_axis[j][0])
+            near = g1near.at[j, side, p]
+            arrived(half(near, 1 - side), s1sem.at[j, k, 2 + side], ssem.at[0], first_axis[j][0])
+            arrived(half(near, side), s1sem.at[j, k, 4 + side], ssem.at[0], first_axis[j][0])
         r = prim[j]
         gsum[j, r, p] = (
             gsum[j, r, p].astype(F32) + g1near[j, 0, p].astype(F32) + g1near[j, 1, p].astype(F32)
@@ -571,90 +595,114 @@
                 second_axis[j][side],
             )
 
-    def second_near_send(j):
-        for side, step in enumerate((1, 3)):
-            p = (sec[j] + step) % 4
-            arrived(g2far.at[j, side], s2sem.at[j, side], ssem.at[0], second_axis[j][0])
-            rows = pl.ds(128 * side, 128)
-            gsum[j, prim[j], p, rows] = (
-                gsum[j, prim[j], p, rows].astype(F32) + g2far[j, side].astype(F32)
-            ).astype(BF)
-            out.start(
-                gsum.at[j, prim[j], p], g2near.at[j, side], s2sem.at[j, 2 + side],
-                second_axis[j][side],
-            )
+    def second_fresh(j, side):
+        p = (sec[j] + (1, 3)[side]) % 4
+        out.start(
+            half(gsum.at[j, prim[j], p], 1 - side), half(g2near.at[j, side], 1 - side),
+            s2sem.at[j, 2 + side], second_axis[j][side],
+        )
+
+    def second_relay(j, side):
+        p = (sec[j] + (1, 3)[side]) % 4
+        arrived(g2far.at[j, side], s2sem.at[j, side], ssem.at[0], second_axis[j][0])
+        add(gsum, (j, prim[j], p, pl.ds(128 * side, 128)), g2far[j, side])
+        out.start(
+            half(gsum.at[j, prim[j], p], side), half(g2near.at[j, side], side),
+            s2sem.at[j, 4 + side], second_axis[j][side],
+        )
 
     def second_final(j, result):
         for side in (0, 1):
-            arrived(g2near.at[j, side], s2sem.at[j, 2 + side], ssem.at[0], second_axis[j][0])
+            near = g2near.at[j, side]
+            arrived(half(near, 1 - side), s2sem.at[j, 2 + side], ssem.at[0], second_axis[j][0])
+            arrived(half(near, side), s2sem.at[j, 4 + side], ssem.at[0], second_axis[j][0])
         result[...] = jnp.transpose(
             gsum[j, prim[j], sec[j]].astype(F32)
             + g2near[j, 0].astype(F32)
             + g2near[j, 1].astype(F32)
         )
 
-    def z_send(step):
-        if step == 0:
-            zd = (z + 4) % 8
-            for side, onward in enumerate((up, down)):
-                out.start(
-                    rows256(tme.at[zd], side), rows256(zgot.at[side, 0], side), rzsem.at[side, 0],
-                    onward,
-                )
-            return
-        for side, (zd, onward) in enumerate((((z + 4 - step) % 8, up), ((z + 4 + step) % 8, down))):
-            if step == 1:
-                rows = pl.ds(256 * side, 256)
-                arrived(zgot.at[side, 0, rows], rzsem.at[side, 0], ssem.at[0], up)
-                tme[zd, rows] = (
-                    tme[zd, rows].astype(F32) + zgot[side, 0, rows].astype(F32)
-                ).astype(BF)
-            else:
-                arrived(zgot.at[side, step - 1], rzsem.at[side, step - 1], ssem.at[0], up)
-                tme[zd] = (tme[zd].astype(F32) + zgot[side, step - 1].astype(F32)).astype(BF)
-            out.start(tme.at[zd], zgot.at[side, step], rzsem.at[side, step], onward)
+    def z_start(side, step, k):
+        zd = (z + 4 - step) % 8 if side == 0 else (z + 4 + step) % 8
+        out.start(
+            rows256(tme.at[zd], k), rows256(zgot.at[side, step], k), rzsem.at[side, step, k],
+            (up, down)[side],
+        )
+
+    def z_relay(step, own):
+        for side in (0, 1):
+            k = side if own else 1 - side
+            zd = (z + 4 - step) % 8 if side == 0 else (z + 4 + step) % 8
+            rows = pl.ds(256 * k, 256)
+            arrived(zgot.at[side, step - 1, rows], rzsem.at[side, step - 1, k], ssem.at[0], up)
+            add(tme, (zd, rows), zgot[side, step - 1, rows])
+            z_start(side, step, k)
 
     zorder = [(z + off) % 8 for off in (4, 3, 5, 2, 6, 1, 7, 0)]
 
-    twin_term(0, zorder[0])
-    for j in (0, 1):
-        grads(j, (prim[j] + 2) % 4)
-        first_far_send(j)
-    my_term(zorder[0])
-    pair(0, zorder[0])
-    z_send(0)
-    for k in (1, 2):
+    def both_terms(k):
         twin_term(k, zorder[k])
         my_term(zorder[k])
-    for j in (0, 1):
-        grads(j, (prim[j] + 1) % 4)
-        grads(j, (prim[j] + 3) % 4)
-        first_near_send(j)
+
+    twin_term(0, zorder[0])
+    for j in (0, 1):
+        grads(j, offs[0])
+        first_sends(j, 0)
+    my_term(zorder[0])
+    both_terms(1)
+    both_terms(2)
+    pair(0, zorder[0])
+    for side in (0, 1):
+        z_start(side, 0, side)
+    for j in (0, 1):
+        grads(j, offs[1])
+        first_sends(j, 1)
     pair(1, zorder[1])
     pair(2, zorder[2])
-    z_send(1)
-    for k in (3, 4, 5, 6, 7):
-        twin_term(k, zorder[k])
-        my_term(zorder[k])
-    for j in (0, 1):
-        grads(j, prim[j])
+    for side in (0, 1):
+        z_start(side, 1, 1 - side)
+    for k in (2, 3):
+        for j in (0, 1):
+            grads(j, offs[k])
+            first_sends(j, k)
+    both_terms(3)
+    both_terms(4)
+    for j in (0, 1):
+        first_relay(j, 0)
+    z_relay(1, True)
+    for j in (0, 1):
+        first_relay(j, 1)
+        own_grads(j)
+    both_terms(5)
+    both_terms(6)
     pair(3, zorder[3])
     pair(4, zorder[4])
-    z_send(2)
+    z_relay(2, False)
+    for j in (0, 1):
+        first_relay(j, 2)
+        first_relay(j, 3)
+    both_terms(7)
+    z_relay(2, True)
     for j in (0, 1):
         first_final(j, 0)
         second_far_send(j)
     pair(5, zorder[5])
     pair(6, zorder[6])
-    z_send(3)
-    for j in (0, 1):
-        first_final(j, 1)
-        first_final(j, 2)
-        second_near_send(j)
+    z_relay(3, False)
+    for side in (0, 1):
+        for j in (0, 1):
+            first_final(j, 1 + side)
+            second_fresh(j, side)
+    z_relay(3, True)
+    for j in (0, 1):
+        for side in (0, 1):
+            second_relay(j, side)
+    pair(7, zorder[7])
+    for j in (0, 1):
         first_final(j, 3)
-    pair(7, zorder[7])
     for side in (0, 1):
-        arrived(zgot.at[side, 3], rzsem.at[side, 3], ssem.at[0], up)
+        for k in (1 - side, side):
+            arrived(rows256(zgot.at[side, 3], k), rzsem.at[side, 3, k], ssem.at[0], up)
     ig[...] = (
         tme[z].astype(F32) + zgot[0, 3].astype(F32) + zgot[1, 3].astype(F32)
     ).astype(BF)
@@ -738,15 +786,15 @@
             V((2, 2, 256, 256), BF),
             pltpu.SemaphoreType.DMA((13,)),
             pltpu.SemaphoreType.DMA((13,)),
-            pltpu.SemaphoreType.DMA((160,)),
+            pltpu.SemaphoreType.DMA((176,)),
             pltpu.SemaphoreType.DMA((2, 4, 2)),
             pltpu.SemaphoreType.DMA((2, 5)),
             pltpu.SemaphoreType.DMA((2, 4)),
             pltpu.SemaphoreType.DMA((2, 4, 4)),
             pltpu.SemaphoreType.DMA((8,)),
-            pltpu.SemaphoreType.DMA((2, 4)),
-            pltpu.SemaphoreType.DMA((2, 4, 4)),
-            pltpu.SemaphoreType.DMA((2, 4)),
+            pltpu.SemaphoreType.DMA((2, 4, 2)),
+            pltpu.SemaphoreType.DMA((2, 4, 6)),
+            pltpu.SemaphoreType.DMA((2, 6)),
         ],
         compiler_params=pltpu.CompilerParams(
             collective_id=0, has_side_effects=True, vmem_limit_bytes=63 * 1024 * 1024

time: 143 us -> 139 us (0.972)
  Pallas kernels: 142 us -> 137 us
    pallas_call x1, Pallas kernels: 140 us -> 135 us  [per_device(): pl.pallas_call(whole_kernel, out_shape=shapes, in_specs=[vm] * 6, out_spe...]
where the time goes in v1:
time: 139 us; the launch traced here: 137 us
  Pallas kernels  137 us (99%)
    pallas_call x1, Pallas kernels, per_device(): pl.pallas_call(whole_kernel, out_shape=shapes, in_specs=[vm] * 6, out_spe...  135 us

profile of v1, /device:TPU:8, one launch (start us, length us, event | category | flops | bytes accessed | tf_op | source)
XLA Modules:
  0.0 137.4 jit_solution(2404434850667602024)
XLA Ops:
  0.6 134.6 %hashed_attention_step.1 = (bf16[512,256]{1,0:T(8,128)(2,1)}, bf16[512,256]{1,0:T(8,128)(2,1)}, f32[256,256]{1,0:T(8,128)}, f32[256,256]{1,0:T(8,128)}) custom-call(bf16[512,256]{1,0:T(8,128)(2,1)} %x_ref.1, bf16[256,256]{1,0:T(8,128)(2,1)} %wq_ref.1, bf16[256,256]{1,0:T(8,128)(2,1)} %wv_ref.1, bf16[512,256]{1,0:T(8,128)(2,1)} %dout.1, ...), custom_call_target="tpu_custom_call" | custom-call | tf_op jit(solution)/shard_map/hashed_attention_step/pallas_call | solution.py:735
  135.3 2.2 %write_results.1 = (bf16[512,256]{1,0:T(8,128)(2,1)}, bf16[512,256]{1,0:T(8,128)(2,1)}, f32[256,256]{1,0:T(8,128)}, f32[256,256]{1,0:T(8,128)}) custom-call(bf16[512,256]{1,0:T(8,128)(2,1)} %get-tuple-element.8.refs_0_, bf16[512,256]{1,0:T(8,128)(2,1)} %get-tuple-element.9.refs_1_, f32[256,256]{1,0:T(8,128)} %get-tuple-element.10.refs_2_, ...), custom_call_target="tpu_custom_call" | custom-call | tf_op jit(solution)/shard_map/write_results/pallas_call | solution.py:804

commit v2 on v1

--- a/solution.py
+++ b/solution.py
@@ -99,17 +99,25 @@
 
 
 def whole_kernel(
-    x_ref, wq_ref, wv_ref, dout, grow, brow,
+    x_ref, wq_ref, wv_ref, dout_ref, grow, brow,
     output, ig, gq, gv,
-    xg, wg, dqv, dqvt,
+    xg, wg, dqv, dqvt, dout,
     qv, pick, unpick, order, unorder, live, hot, rk,
     kbuf, kgot, sbuf, rbuf, dbuf, dgot, obuf, ogot, ggot, lbuf, lgot, mbuf, mgot,
-    qs, ks, vs, ds_, probs, pairs, osum, vals, slots, dks, dvs, mixes,
+    qs, ks, vs, ds_, probs, pairs, osum, vals, slots, mixes,
     tme, ttwin, tgot, zgot, gsum, g1far, g1near, g2far, g2near,
-    asend, arecv, ssem, zsem, tsem, w1sem, w2sem, rtsem, rzsem, s1sem, s2sem,
+    lsem, asend, arecv, ssem, zsem, tsem, w1sem, w2sem, rtsem, rzsem, s1sem, s2sem,
 ):
     s, h, x, y, z, c = place()
     east, west, north, south, up, down, twin = ring_neighbours()
+    local = [
+        pltpu.make_async_copy(x_ref, xg.at[h], lsem.at[0]),
+        pltpu.make_async_copy(wq_ref, wg.at[s, 0], lsem.at[1]),
+        pltpu.make_async_copy(wv_ref, wg.at[s, 1], lsem.at[2]),
+        pltpu.make_async_copy(dout_ref, dout, lsem.at[3]),
+    ]
+    for copy in local:
+        copy.start()
     barrier = pltpu.get_barrier_semaphore()
 
     @pl.loop(1, 16)
@@ -231,9 +239,6 @@
             ref = xg.at[((z + 4) % 8) * 2 + 1 - c]
             arrived(rows256(ref, side), tsem.at[side, 4], ssem.at[0], twin)
 
-    xg[h] = x_ref[...]
-    wg[s, 0] = wq_ref[...]
-    wg[s, 1] = wv_ref[...]
 
     kbuf[...] = jnp.zeros_like(kbuf)
     lbuf[...] = jnp.zeros_like(lbuf)
@@ -305,6 +310,8 @@
         second_arrivals(j, 1)
     z_arrival(2)
     pick[1] = onehot(iota((768, 512), 0) == slot_rows[1])
+    for copy in local:
+        copy.wait()
     for t in (0, 1):
         dbuf[:, t] = mm(pick[t], dout[...], 1, 0).astype(BF).reshape(16, 48, 256)
 
@@ -377,27 +384,29 @@
             qs[u] = qf.astype(BF)
             ks[u] = (qf * fac).astype(BF)
             vs[u] = rows[:, 128:256].astype(BF)
+            used = jnp.concatenate([live[t, 0:1, :]] * 2, axis=1)
+            parts = []
             for b in range(6):
                 prev = (b + 5) % 6
                 at = iota((1, 256), 1)
                 at = jnp.where(at < 128.0, at + 128.0 * b, at - 128.0 + 128.0 * prev)
-                used = jnp.concatenate([live[t, 0:1, :]] * 2, axis=1)
-                scores = mm(qs[u, 128 * b:128 * (b + 1)], both(ks, u, b), 1, 1)
-                scores = jnp.where(self_pair, SELF_SCORE, scores)
-                scores = jnp.where(at < used, scores, MASKED_SCORE)
-                top = jnp.max(scores, axis=1, keepdims=True)
-                e = jnp.exp(scores - top)
-                total = jnp.sum(e, axis=1, keepdims=True)
-                weights = e * (1.0 / total)
-                probs[u, b] = weights
-                mixed = mm(weights.astype(BF), both(vs, u, b), 1, 0)
-                osum[u, 128 * b:128 * (b + 1)] = mixed
-                grad = ds_[u, 128 * b:128 * (b + 1)]
-                pairs[u, b] = mm(grad, both(vs, u, b), 1, 1)
-                vals[t, 128 * b:128 * (b + 1), 2 + n:3 + n] = jnp.sum(
-                    grad.astype(F32) * mixed, axis=1, keepdims=True
-                )
-                vals[t, 128 * b:128 * (b + 1), n:n + 1] = top + jnp.log(total)
+                part = mm(qs[u, 128 * b:128 * (b + 1)], both(ks, u, b), 1, 1)
+                part = jnp.where(self_pair, SELF_SCORE, part)
+                parts.append(jnp.where(at < used, part, MASKED_SCORE))
+                pairs[u, b] = mm(ds_[u, 128 * b:128 * (b + 1)], both(vs, u, b), 1, 1)
+            scores = jnp.concatenate(parts, axis=0)
+            top = jnp.max(scores, axis=1, keepdims=True)
+            e = jnp.exp(scores - top)
+            total = jnp.sum(e, axis=1, keepdims=True)
+            weights = e * (1.0 / total)
+            probs[u] = weights.reshape(6, 128, 256)
+            packed = weights.astype(BF)
+            mixed = jnp.concatenate(
+                [mm(packed[128 * b:128 * (b + 1)], both(vs, u, b), 1, 0) for b in range(6)], axis=0
+            )
+            osum[u] = mixed
+            vals[t, :, n:n + 1] = top + jnp.log(total)
+            vals[t, :, 2 + n:3 + n] = jnp.sum(ds_[u].astype(F32) * mixed, axis=1, keepdims=True)
             if n == 1:
                 high, mid, low = split3(vals[t])
                 lines = pieces(
@@ -414,8 +423,6 @@
     for t in (0, 1):
         wide = jnp.concatenate([osum[t], osum[2 + t]], axis=1).astype(BF)
         obuf[:, t] = mm(unorder[t], wide, 1, 0).astype(BF).reshape(16, 48, 256)
-    post(7, obuf, ogot)
-
     collect(6, lgot)
     here = []
     for t in (0, 1):
@@ -443,6 +450,7 @@
             mbuf[g, 8 * t:8 * (t + 1), :] = fold3(back[24 * g:24 * (g + 1)], 8)
         mix_lines.append(split)
     post(8, mbuf, mgot)
+    post(7, obuf, ogot)
     for t in (0, 1):
         mixes[t] = mm(onehot(eye), mix_lines[t].astype(BF), 1, 1)
 
@@ -466,29 +474,27 @@
             sent(1 + u, sbuf.at[n, t])
             mix_col = column(vals, t, n)
             inner_col = column(vals, t, 2 + n)
-            dks[...] = jnp.zeros_like(dks)
-            dvs[...] = jnp.zeros_like(dvs)
-            dq = []
-            for b in range(6):
-                prev = (b + 5) % 6
-                rows = slice(128 * b, 128 * (b + 1))
-                prows = slice(128 * prev, 128 * (prev + 1))
-                weighted = probs[u, b] * mix_col[rows]
-                grads = jnp.where(self_pair, 0.0, weighted * (pairs[u, b] - inner_col[rows]))
-                grads = grads.astype(BF)
-                dq.append(mm(grads, both(ks, u, b), 1, 0))
-                dk = mm(grads, qs[u, rows], 0, 0)
-                dv = mm(weighted.astype(BF), ds_[u, rows], 0, 0)
-                dks[rows] += dk[0:128]
-                dks[prows] += dk[128:256]
-                dvs[rows] += dv[0:128]
-                dvs[prows] += dv[128:256]
+            weighted = probs[u].reshape(768, 256) * mix_col
+            grads = weighted * (pairs[u].reshape(768, 256) - inner_col)
+            self_all = jnp.concatenate([jnp.where(self_pair, 0.0, 1.0)] * 6, axis=0)
+            grads = jnp.where(self_all == 0.0, 0.0, grads).astype(BF)
+            weighted = weighted.astype(BF)
+            blocks = [slice(128 * b, 128 * (b + 1)) for b in range(6)]
+            dq = [mm(grads[blocks[b]], both(ks, u, b), 1, 0) for b in range(6)]
+            dk = [mm(grads[blocks[b]], qs[u, blocks[b]], 0, 0) for b in range(6)]
+            dv = [mm(weighted[blocks[b]], ds_[u, blocks[b]], 0, 0) for b in range(6)]
+
+            def folded(grad):
+                return jnp.concatenate(
+                    [grad[b][0:128] + grad[(b + 1) % 6][128:256] for b in range(6)], axis=0
+                )
+
             qf = qs[u].astype(F32)
             fac = key_factor(qf)
-            dk = dks[...]
+            dk = folded(dk)
             inside = jnp.sum(dk * qf, axis=1, keepdims=True)
             result = jnp.concatenate(dq, axis=0) + fac * dk - fac * fac * fac * inside * qf
-            wide = jnp.concatenate([result.astype(BF), dvs[...].astype(BF)], axis=1)
+            wide = jnp.concatenate([result.astype(BF), folded(dv).astype(BF)], axis=1)
             sbuf[n, t] = mm(unorder[t], wide, 1, 0).astype(BF).reshape(16, 48, 256)
             post(9 + u, sbuf.at[n, t], ggot.at[n, t])
 
@@ -532,9 +538,9 @@
     def grads(j, off):
         p = (sec[j] + off) % 4
 
-        @pl.loop(1, 4)
+        @pl.loop(0, 2)
         def _(i):
-            r = (prim[j] + i) % 4
+            r = (prim[j] + 2 * i + 1) % 4
             b = r * 4 + p if j == 0 else p * 4 + r
             gsum[j, r, p] = mm(dqvt[256 * j:256 * (j + 1), :], xg[b], 1, 0).astype(BF)
 
@@ -550,14 +556,19 @@
     def add(ref, index, other):
         ref[index] = (ref[index].astype(F32) + other.astype(F32)).astype(BF)
 
-    def first_sends(j, k):
+    def first_far_sends(j, k):
         p = (sec[j] + offs[k]) % 4
         r = (prim[j] + 2) % 4
+        b = r * 4 + p if j == 0 else p * 4 + r
+        gsum[j, r, p] = mm(dqvt[256 * j:256 * (j + 1), :], xg[b], 1, 0).astype(BF)
         for side in (0, 1):
             out.start(
                 half(gsum.at[j, r, p], side), g1far.at[j, side, p], s1sem.at[j, k, side],
                 first_axis[j][side],
             )
+
+    def first_sends(j, k):
+        p = (sec[j] + offs[k]) % 4
         for side, step in enumerate((1, 3)):
             r = (prim[j] + step) % 4
             out.start(
@@ -646,6 +657,8 @@
 
     twin_term(0, zorder[0])
     for j in (0, 1):
+        first_far_sends(j, 0)
+    for j in (0, 1):
         grads(j, offs[0])
         first_sends(j, 0)
     my_term(zorder[0])
@@ -655,6 +668,7 @@
     for side in (0, 1):
         z_start(side, 0, side)
     for j in (0, 1):
+        first_far_sends(j, 1)
         grads(j, offs[1])
         first_sends(j, 1)
     pair(1, zorder[1])
@@ -663,6 +677,7 @@
         z_start(side, 1, 1 - side)
     for k in (2, 3):
         for j in (0, 1):
+            first_far_sends(j, k)
             grads(j, offs[k])
             first_sends(j, k)
     both_terms(3)
@@ -735,13 +750,14 @@
     results = pl.pallas_call(
         whole_kernel,
         out_shape=shapes,
-        in_specs=[vm] * 6,
+        in_specs=[pl.BlockSpec(memory_space=pl.ANY)] * 4 + [vm] * 2,
         out_specs=(vm,) * 4,
         scratch_shapes=[
             V((16, 512, 256), BF),
             V((16, 2, 256, 256), BF),
             V((512, 512), BF),
             V((512, 512), BF),
+            V((512, 256), BF),
             V((2, 512, 256), BF),
             V((2, 768, 512), BF),
             V((512, 1536), BF),
@@ -772,8 +788,6 @@
             V((4, 768, 128), F32),
             V((2, 768, 128), F32),
             V((2, 768, 128), BF),
-            V((768, 128), F32),
-            V((768, 128), F32),
             V((2, 512, 24), F32),
             V((8, 512, 256), BF),
             V((8, 512, 256), BF),
@@ -784,6 +798,7 @@
             V((2, 2, 4, 256, 256), BF),
             V((2, 2, 128, 256), BF),
             V((2, 2, 256, 256), BF),
+            pltpu.SemaphoreType.DMA((4,)),
             pltpu.SemaphoreType.DMA((13,)),
             pltpu.SemaphoreType.DMA((13,)),
             pltpu.SemaphoreType.DMA((176,)),

time: 139 us -> 135 us (0.971); the launches traced: 137 us -> 135 us
  Pallas kernels: 137 us -> 134 us
    pallas_call x1, Pallas kernels: 135 us -> 132 us  [per_device(): pl.pallas_call(whole_kernel, out_shape=shapes, in_specs=[pl.BlockSpec(mem...]
where the time goes in v2:
time: 135 us
  Pallas kernels  134 us (99%)
    pallas_call x1, Pallas kernels, per_device(): pl.pallas_call(whole_kernel, out_shape=shapes, in_specs=[pl.BlockSpec(mem...  132 us

profile of v2, /device:TPU:8, one launch (start us, length us, event | category | flops | bytes accessed | tf_op | source)
XLA Modules:
  0.0 135.0 jit_solution(6176858796998790836)
XLA Ops:
  0.6 132.2 %hashed_attention_step.1 = (bf16[512,256]{1,0:T(8,128)(2,1)}, bf16[512,256]{1,0:T(8,128)(2,1)}, f32[256,256]{1,0:T(8,128)}, f32[256,256]{1,0:T(8,128)}) custom-call(bf16[512,256]{1,0:T(8,128)(2,1)} %x_ref.1, bf16[256,256]{1,0:T(8,128)(2,1)} %wq_ref.1, bf16[256,256]{1,0:T(8,128)(2,1)} %wv_ref.1, bf16[512,256]{1,0:T(8,128)(2,1)} %dout_ref.1, ...), custom_call_target="tpu_custom_call" | custom-call | tf_op jit(solution)/shard_map/hashed_attention_step/pallas_call | solution.py:750
  132.8 2.2 %write_results.1 = (bf16[512,256]{1,0:T(8,128)(2,1)}, bf16[512,256]{1,0:T(8,128)(2,1)}, f32[256,256]{1,0:T(8,128)}, f32[256,256]{1,0:T(8,128)}) custom-call(bf16[512,256]{1,0:T(8,128)(2,1)} %get-tuple-element.8.refs_0_, bf16[512,256]{1,0:T(8,128)(2,1)} %get-tuple-element.9.refs_1_, f32[256,256]{1,0:T(8,128)} %get-tuple-element.10.refs_2_, ...), custom_call_target="tpu_custom_call" | custom-call | tf_op jit(solution)/shard_map/write_results/pallas_call | solution.py:819

commit v3 on v2

--- a/solution.py
+++ b/solution.py
@@ -414,10 +414,11 @@
                     + mm(choose, mid.astype(BF), 1, 1)
                     + mm(choose, low.astype(BF), 1, 1)
                 )
+                placed = fold3(mm(lines, order[t], 1, 0), 8)
                 for d in range(16):
-                    lbuf[d, pl.ds(pl.multiple_of(8 * t, 8), 8), 0:48] = fold3(
-                        mm(lines, unorder[t, 48 * d:48 * (d + 1)], 1, 1), 8
-                    )
+                    lbuf[d, pl.ds(pl.multiple_of(8 * t, 8), 8), 0:48] = placed[
+                        :, 48 * d:48 * (d + 1)
+                    ]
 
     post(6, lbuf, lgot)
     for t in (0, 1):

time: 135 us -> 136 us (level); the launches traced: 135 us -> 134 us
  no operation moved by 1% of the time
where the time goes in v3:
time: 136 us; the launch traced here: 134 us
  Pallas kernels  134 us (99%)
    pallas_call x1, Pallas kernels, per_device(): pl.pallas_call(whole_kernel, out_shape=shapes, in_specs=[pl.BlockSpec(mem...  132 us

profile of v3, /device:TPU:8, one launch (start us, length us, event | category | flops | bytes accessed | tf_op | source)
XLA Modules:
  0.0 134.5 jit_solution(7976906072796093410)
XLA Ops:
  0.6 131.7 %hashed_attention_step.1 = (bf16[512,256]{1,0:T(8,128)(2,1)}, bf16[512,256]{1,0:T(8,128)(2,1)}, f32[256,256]{1,0:T(8,128)}, f32[256,256]{1,0:T(8,128)}) custom-call(bf16[512,256]{1,0:T(8,128)(2,1)} %x_ref.1, bf16[256,256]{1,0:T(8,128)(2,1)} %wq_ref.1, bf16[256,256]{1,0:T(8,128)(2,1)} %wv_ref.1, bf16[512,256]{1,0:T(8,128)(2,1)} %dout_ref.1, ...), custom_call_target="tpu_custom_call" | custom-call | tf_op jit(solution)/shard_map/hashed_attention_step/pallas_call | solution.py:751
  132.3 2.2 %write_results.1 = (bf16[512,256]{1,0:T(8,128)(2,1)}, bf16[512,256]{1,0:T(8,128)(2,1)}, f32[256,256]{1,0:T(8,128)}, f32[256,256]{1,0:T(8,128)}) custom-call(bf16[512,256]{1,0:T(8,128)(2,1)} %get-tuple-element.8.refs_0_, bf16[512,256]{1,0:T(8,128)(2,1)} %get-tuple-element.9.refs_1_, f32[256,256]{1,0:T(8,128)} %get-tuple-element.10.refs_2_, ...), custom_call_target="tpu_custom_call" | custom-call | tf_op jit(solution)/shard_map/write_results/pallas_call | solution.py:820
